TPU v7x, 32 devices: a whole 2x2x4 slice. The times are simulated.
32 devices in a mesh: leaf: 8 (over z, core), sub: 4 (over y, x).
Axes of the slice: x: 2, y: 2, z: 4, core: 2. Of those that a mesh axis runs over, the one named last changes fastest.
Arguments:
- leaf_maps: float32 [32, 256, 1024], P('leaf', 'sub'), may hold values from -8 to 28, as said below
- order_one: int32 [8, 4], replicated, may hold values from 0 to 3, each once within a row
- order_two: int32 [4, 6], replicated, may hold values from 0 to 5, each once within a row
- top_data: float32 [16, 256, 256], P('leaf', 'sub'), may hold values from -6 to 6
Outputs:
- top_map: float32 [16, 256, 2048], P('leaf', 'sub')
- leaf_data: float32 [32, 256, 256], P('leaf', 'sub')
Inputs may be any that keep to these rules, and one draw needn't show every extreme that they name: Each leaf's block of 1024 rows of leaf_maps, read as a 1024 by 1024 matrix, is symmetric and positive definite.
All inputs are finite; a program needn't handle non-finite values. Where the computation divides by a largest or mean magnitude, that divisor is 1e-20 or more.
Results may differ from a plain program's by a relative error of at most 0.0001.
Values sent between devices are 32-bit elements; how exact they have to be, the bound alone decides.
No kernel may reach another device: no remote copies, remote signals or barrier semaphores. Data moves between devices by JAX's collectives and lax.ppermute only.
A program may use at most 64 MiB of HBM per device.

v0:
```python
import jax
import jax.numpy as jnp
from jax import lax
from jax.sharding import PartitionSpec as P

W = 256
K = 256
NS_STEPS = 4


def swapped(value, axis, apart):
    mask = 2**apart
    pairs = [(source, source ^ mask) for source in range(lax.axis_size(axis))]
    return lax.ppermute(value, axis, pairs)


def exact_dot(left_matrix, right_matrix):
    return jnp.dot(
        left_matrix,
        right_matrix,
        precision=lax.Precision.HIGHEST,
        preferred_element_type=jnp.float32,
    )


def interface_inverse(block_rows):
    slot_count, width_local, block_size = block_rows.shape
    full_block = lax.all_gather(block_rows, "sub", axis=1, tiled=True).reshape(
        block_size, block_size
    )
    row_bound = jnp.max(jnp.sum(jnp.abs(full_block), axis=1))
    iterate = jnp.eye(block_size, dtype=jnp.float32) / row_bound
    for iteration in range(NS_STEPS):
        iterate = 2.0 * iterate - exact_dot(exact_dot(full_block, iterate), iterate)
    return iterate


def shards(leaf_maps, order_one, order_two, top_data):
    width_local = leaf_maps.shape[1]
    group_index = lax.axis_index("leaf")
    member_index = lax.axis_index("sub")
    parity = group_index % 2
    is_first = parity == 0
    own_order = order_one[group_index]
    permuted = jnp.take(leaf_maps, own_order, axis=0)
    permuted = jnp.take(permuted.reshape(4, width_local, 4, W), own_order, axis=2).reshape(
        4, width_local, 4 * W
    )
    near_rows = permuted[:3]
    inner_piece = permuted[3]
    other_piece = swapped(inner_piece, "leaf", 0)
    first_piece = jnp.where(is_first, inner_piece, other_piece)
    second_piece = jnp.where(is_first, other_piece, inner_piece)
    block_one = first_piece[:, 3 * W :] + second_piece[:, 3 * W :]
    inverse_one = interface_inverse(block_one[None])
    coupling_one = near_rows[:, :, 3 * W :].reshape(3 * width_local, W)
    scaled_one = exact_dot(coupling_one, inverse_one)
    pieces = (
        lax.all_gather(first_piece[:, : 3 * W], "sub", axis=0, tiled=True),
        lax.all_gather(second_piece[:, : 3 * W], "sub", axis=0, tiled=True),
    )
    piece_rows = pieces[0].shape[0]
    joined = jnp.concatenate([pieces[0], pieces[1]], axis=1)
    coeff_part = scaled_one
    running_sum = exact_dot(coeff_part, joined)
    own_part = jnp.where(is_first, pieces[0], pieces[1]).reshape(piece_rows, 3, W)
    own_part = lax.dynamic_slice_in_dim(own_part, member_index * width_local, width_local, 2)
    kept_columns = own_part.reshape(piece_rows, 3 * width_local)
    product_one = running_sum
    right_one = kept_columns
    own_outer = near_rows[:, :, : 3 * W].reshape(3 * width_local, 3 * W)
    zero_one = jnp.zeros_like(own_outer)
    diagonal_one = jnp.where(
        is_first,
        jnp.concatenate([own_outer, zero_one], axis=1),
        jnp.concatenate([zero_one, own_outer], axis=1),
    )
    merged_one = (diagonal_one - product_one).reshape(3, width_local, 6 * W)
    node_index = group_index // 2
    node_first = node_index % 2 == 0
    node_order = order_two[node_index]
    node_rows = jnp.take(merged_one.reshape(3, width_local, 6, W), node_order, axis=2).reshape(
        3, width_local, 6 * W
    )
    position_table = jnp.sum(
        jnp.arange(6)[:, None] * (node_order[:, None] == jnp.arange(6)[None, :]).astype(jnp.int32),
        axis=0,
    )
    my_positions = jnp.take(position_table, 3 * parity + jnp.arange(3))
    slot_edges = node_order[4:6]
    slot_held = (slot_edges // 3 == parity).astype(jnp.float32)
    slot_piece = jnp.take(node_rows, slot_edges % 3, axis=0) * slot_held[:, None, None]
    node_piece = slot_piece + swapped(slot_piece, "leaf", 0)
    cousin_piece = swapped(node_piece, "leaf", 1)
    first_node = jnp.where(node_first, node_piece, cousin_piece)
    second_node = jnp.where(node_first, cousin_piece, node_piece)
    block_two = first_node[:, :, 4 * W :] + second_node[:, :, 4 * W :]
    inverse_two = interface_inverse(block_two)
    coupling_two = node_rows[:, :, 4 * W :].reshape(3 * width_local, 2 * W)
    scaled_two = exact_dot(coupling_two, inverse_two).reshape(3 * width_local, 2, W)
    top_first = 2 * (group_index % 4)
    pieces = (
        lax.all_gather(first_node[:, :, : 4 * W], "sub", axis=1, tiled=True),
        lax.all_gather(second_node[:, :, : 4 * W], "sub", axis=1, tiled=True),
    )
    piece_rows = pieces[0].shape[1]
    joined = jnp.concatenate([pieces[0], pieces[1]], axis=2)
    coeff_part = scaled_two.reshape(3 * width_local, 2 * piece_rows)
    running_sum = exact_dot(coeff_part, joined.reshape(2 * piece_rows, 8 * W))
    own_part = lax.dynamic_slice_in_dim(joined.reshape(2, piece_rows, 8, W), top_first, 2, 2)
    own_part = lax.dynamic_slice_in_dim(own_part, member_index * width_local, width_local, 3)
    kept_columns = own_part
    node_outer = node_rows[:, :, : 4 * W].reshape(3 * width_local, 4 * W)
    zero_two = jnp.zeros_like(node_outer)
    diagonal_two = jnp.where(
        node_first,
        jnp.concatenate([node_outer, zero_two], axis=1),
        jnp.concatenate([zero_two, node_outer], axis=1),
    )
    top_rows = (diagonal_two - running_sum).reshape(3, width_local, 8 * W)
    node_offset = 4 * (node_index % 2)
    buffer = jnp.zeros((8, width_local, 8 * W), jnp.float32)
    for row_slot in range(3):
        target = node_offset + my_positions[row_slot]
        marker = ((jnp.arange(8) == target) & (my_positions[row_slot] < 4)).astype(jnp.float32)
        buffer = buffer + marker[:, None, None] * top_rows[row_slot][None]
    upper_half = node_index % 2
    outgoing = lax.dynamic_slice_in_dim(buffer, 4 * (1 - upper_half), 4, 0)
    retained = lax.dynamic_slice_in_dim(buffer, 4 * upper_half, 4, 0)
    retained = retained + swapped(outgoing, "leaf", 1)
    outgoing_near = lax.dynamic_slice_in_dim(retained, 2 * (1 - parity), 2, 0)
    own_part = lax.dynamic_slice_in_dim(retained, 2 * parity, 2, 0)
    top_map = own_part + swapped(outgoing_near, "leaf", 0)
    partial_two = exact_dot(
        kept_columns.reshape(2 * W, 2 * width_local), top_data.reshape(2 * width_local, K)
    )
    partial_two = lax.psum(partial_two, "sub")
    spread = lax.dynamic_update_slice_in_dim(
        jnp.zeros((8, width_local, K), jnp.float32), top_data, top_first, 0
    )
    for bit_index in range(2):
        other_sum, other_spread = swapped((partial_two, spread), "leaf", bit_index)
        partial_two = partial_two + other_sum
        spread = spread + other_spread
    inner_two = -exact_dot(inverse_two, partial_two)
    inner_local = lax.dynamic_slice_in_dim(
        inner_two.reshape(2, W, K), member_index * width_local, width_local, 1
    )
    candidates = jnp.concatenate(
        [lax.dynamic_slice_in_dim(spread, node_offset, 4, 0), inner_local], axis=0
    )
    node_data = jnp.take(candidates, my_positions, axis=0)
    partial_one = exact_dot(right_one, node_data.reshape(3 * width_local, K))
    partial_one = lax.psum(partial_one, "sub")
    partial_one = partial_one + swapped(partial_one, "leaf", 0)
    inner_one = -exact_dot(inverse_one, partial_one)
    inner_slice = lax.dynamic_slice_in_dim(inner_one, member_index * width_local, width_local, 0)
    permuted_data = jnp.concatenate([node_data, inner_slice[None]], axis=0)
    restore = (own_order[:, None] == jnp.arange(4)[None, :]).astype(jnp.float32)
    leaf_data = jnp.zeros((4, width_local, K), jnp.float32)
    for position in range(4):
        leaf_data = leaf_data + restore[position][:, None, None] * permuted_data[position][None]
    return (top_map, leaf_data)


def solution(mesh):
    in_specs = (P("leaf", "sub", None), P(), P(), P("leaf", "sub", None))
    out_specs = (P("leaf", "sub", None), P("leaf", "sub", None))
    return jax.shard_map(shards, mesh=mesh, in_specs=in_specs, out_specs=out_specs, check_vma=False)
```

profile of v0, /device:TPU:0, one launch (start us, length us, event | category | flops | bytes accessed | tf_op | source)
XLA Modules:
  0.0 383.9 jit_solution(1197257132475756715)
XLA Ops:
  13.0 10.0 %all-gather = f32[256,256]{1,0:T(8,128)S(1)} all-gather(f32[64,256]{1,0:T(8,128)S(1)} %slice_add_fusion.1), channel_id=2, replica_groups=mesh['leaf'=8,'sub'=4] {'sub'}, dimensions={0}, use_global_device_ids=true | all-gather | bytes 327680 | tf_op jit(solution)/shard_map/all_gather | solution.py:28
  27.6 12.5 %all_gather.20 = f32[256,768]{1,0:T(8,128)S(1)} all-gather(f32[64,768]{1,0:T(8,128)S(1)} %slice.143), channel_id=1, replica_groups=mesh['leaf'=8,'sub'=4] {'sub'}, dimensions={0}, use_global_device_ids=true | all-gather | bytes 983040 | tf_op jit(solution)/shard_map/all_gather | solution.py:60
  40.0 10.2 %all_gather.19 = f32[256,768]{1,0:T(8,128)S(1)} all-gather(f32[64,768]{1,0:T(8,128)S(1)} %slice.142), channel_id=1, replica_groups=mesh['leaf'=8,'sub'=4] {'sub'}, dimensions={0}, use_global_device_ids=true | all-gather | bytes 983040 | tf_op jit(solution)/shard_map/all_gather | solution.py:59
  50.6 1.2 convolution_subtract_fusion
  51.8 1.5 reshape_reshape.3
  53.3 2.8 copy.20
  56.1 1.9 gather_fusion.3
  59.1 2.3 collective-permute-done.1
  61.4 1.0 fusion.90
  62.4 1.6 collective-permute-start.2
  64.0 18.3 %collective-permute-done.2 = f32[2,64,1536]{2,1,0:T(8,128)} collective-permute-done((f32[2,64,1536]{2,1,0:T(8,128)}, f32[2,64,1536]{2,1,0:T(8,128)}, u32[]{:S(2)}, u32[]{:S(2)}) %collective-permute-start.2) | collective-permute-done | bytes 786464 | tf_op jit(solution)/shard_map/ppermute | solution.py:14
  82.3 1.5 broadcast_select_fusion.3
  85.5 1.9 slice.148
  95.5 16.9 %all-gather.5.cloned.1.call-done = f32[2,256,512]{2,1,0:T(8,128)} async-done(((f32[2,64,512]{2,1,0:T(8,128)}), f32[2,256,512]{2,1,0:T(8,128)}) %all-gather.5.cloned.1.call-update) | async-done | bytes 1048592 | tf_op jit(solution)/shard_map/all_gather | solution.py:28
  112.4 1.4 abs_reduce_fusion
  115.1 3.1 fusion.2
  118.2 1.8 fusion.7
  120.0 1.8 fusion.45
  121.8 1.8 convolution_subtract_fusion.4
  123.7 1.8 fusion.46
  125.6 1.8 convolution_subtract_fusion.3
  127.4 2.1 fusion.47
  129.5 1.9 convolution_subtract_fusion.2
  132.3 17.2 %all-gather.7.cloned.1.call-done = f32[2,256,1024]{2,1,0:T(8,128)} async-done(((f32[2,64,1024]{2,1,0:T(8,128)}), f32[2,256,1024]{2,1,0:T(8,128)}) %all-gather.7.cloned.1.call-update) | async-done | bytes 2097168 | tf_op jit(solution)/shard_map/all_gather | solution.py:103
  149.5 3.2 constant_dynamic-update-slice_fusion.1
  152.7 34.4 %all-gather.9.cloned.1.call-done = f32[2,256,1024]{2,1,0:T(8,128)} async-done(((f32[2,64,1024]{2,1,0:T(8,128)}), f32[2,256,1024]{2,1,0:T(8,128)}) %all-gather.9.cloned.1.call-update) | async-done | bytes 2097168 | tf_op jit(solution)/shard_map/all_gather | solution.py:104
  187.1 3.2 constant_dynamic-update-slice_fusion
  190.3 7.3 %copy.24 = f32[2,256,2048]{1,0,2:T(2,128)} copy(f32[2,256,2048]{2,1,0:T(8,128)} %constant_dynamic-update-slice_fusion) | data formatting | bytes 8388608 | tf_op jit(solution)/shard_map/reshape | solution.py:110
  197.6 1.0 constant_dynamic-slice_fusion.1
  198.7 1.4 fusion.49
  200.2 4.7 %convolution_subtract_fusion.1 = f32[192,2048]{1,0:T(8,128)S(1)} fusion(f32[192,512]{1,0:T(8,128)S(1)} %fusion.48, f32[512,2048]{1,0:T(8,128)} %bitcast.129, f32[192,1024]{1,0:T(8,128)S(1)} %bitcast.131, pred[]{:T(512)S(6)} %eq.94), kind=kOutput, calls=%fused_computation.8 | convolution fusion | flops 2416705536 | bytes 6946817 | tf_op jit(solution)/shard_map/dot_general | solution.py:18
  205.8 39.8 %all-reduce.7.cloned.1.call-done = f32[512,256]{1,0:T(8,128)} async-done(((f32[512,256]{1,0:T(8,128)}), f32[512,256]{1,0:T(8,128)}) %all-reduce.7.cloned.1.call-update) | async-done | bytes 524304 | tf_op jit(solution)/shard_map/psum | solution.py:137
  245.6 1.8 multiply_add_fusion
  247.5 1.5 constant_dynamic-slice_fusion.3
  250.0 1.5 collective-permute-start.3
  251.5 1.6 add_dynamic-update-slice_fusion
  254.5 1.5 collective-permute-start.8
  257.0 1.4 copy.23
  258.4 51.7 %collective-permute-done.6 = f32[8,64,256]{2,1,0:T(8,128)} collective-permute-done((f32[8,64,256]{2,1,0:T(8,128)}, f32[8,64,256]{2,1,0:T(8,128)}, u32[]{:S(2)}, u32[]{:S(2)}) %collective-permute-start.6) | collective-permute-done | bytes 524320 | tf_op jit(solution)/shard_map/ppermute | solution.py:14
  310.1 1.1 dynamic-slice_add_fusion.2
  311.1 9.7 %collective-permute-done.8 = f32[512,256]{1,0:T(8,128)} collective-permute-done((f32[512,256]{1,0:T(8,128)}, f32[512,256]{1,0:T(8,128)}, u32[]{:S(2)}, u32[]{:S(2)}) %collective-permute-start.8) | collective-permute-done | bytes 524320 | tf_op jit(solution)/shard_map/ppermute | solution.py:14
  320.9 2.2 convolution_negate_fusion
  323.8 1.4 convolution_bitcast_fusion
  325.3 43.1 %all-reduce.9.cloned.1.call-done = f32[256,256]{1,0:T(8,128)} async-done(((f32[256,256]{1,0:T(8,128)}), f32[256,256]{1,0:T(8,128)}) %all-reduce.9.cloned.1.call-update) | async-done | bytes 262160 | tf_op jit(solution)/shard_map/psum | solution.py:154
  368.4 2.5 dynamic-slice_add_fusion
  370.9 1.0 constant_dynamic-slice_fusion.2
  372.5 1.5 fusion.18
  375.1 2.3 dynamic-slice_add_fusion.1
  (119 shorter events, 24.9 us)
Async XLA Ops:
  7.2 1.2 copy-start
  7.2 105.2 %all-gather.5.cloned.1.call-start = ((), (), s32[]{:S(2)}) async-start(), calls=%async_computation | async-start | bytes 1310720 | tf_op jit(solution)/shard_map/all_gather | solution.py:28
  10.3 2.6 collective-permute-start
  26.8 23.8 %copy-start.8 = (f32[3,64,768]{2,1,0:T(8,128)S(1)}, f32[3,64,768]{2,1,0:T(8,128)}, u32[]{:S(2)}) copy-start(f32[3,64,768]{2,1,0:T(8,128)} %slice.137) | copy-start | bytes 1769476
  50.2 1.6 copy-start.5
  58.3 37.3 %copy-start.4 = (f32[3,64,1536]{2,1,0:T(8,128)}, f32[3,64,1536]{2,1,0:T(8,128)S(1)}, u32[]{:S(2)}) copy-start(f32[3,64,1536]{2,1,0:T(8,128)S(1)} %broadcast_select_fusion) | copy-start | bytes 3538948
  59.0 2.4 collective-permute-start.1
  62.4 19.9 %collective-permute-start.2 = (f32[2,64,1536]{2,1,0:T(8,128)}, f32[2,64,1536]{2,1,0:T(8,128)}, u32[]{:S(2)}, u32[]{:S(2)}) collective-permute-start(f32[2,64,1536]{2,1,0:T(8,128)} %fusion.90), channel_id=1, source_target_pairs={{0,8},{4,12},{8,0},{12,4},{16,24},{20,28},{24,16},{28,20},{1,9},{5... | collective-permute-start | bytes 2359304 | tf_op jit(solution)/shard_map/ppermute | solution.py:14
  83.8 0.9 copy-start.7
  83.8 4.5 %copy-start.9 = (f32[2,64,256]{2,1,0:T(8,128)S(1)}, f32[2,64,256]{2,1,0:T(8,128)}, u32[]{:S(2)}) copy-start(f32[2,64,256]{2,1,0:T(8,128)} %param.7) | copy-start | bytes 393220
  85.5 64.0 %all-gather.7.cloned.1.call-start = ((), (), s32[]{:S(2)}) async-start(), calls=%async_computation.1 | async-start | bytes 2621440 | tf_op jit(solution)/shard_map/all_gather | solution.py:103
  87.5 99.7 %all-gather.9.cloned.1.call-start = ((), (), s32[]{:S(2)}) async-start(), calls=%async_computation.2 | async-start | bytes 2621440 | tf_op jit(solution)/shard_map/all_gather | solution.py:104
  89.0 162.5 %collective-permute-start.5 = (f32[8,64,256]{2,1,0:T(8,128)}, f32[8,64,256]{2,1,0:T(8,128)}, u32[]{:S(2)}, u32[]{:S(2)}) collective-permute-start(f32[8,64,256]{2,1,0:T(8,128)} %constant_dynamic-update-slice_fusion.2), channel_id=1, source_target_pairs={{0,4},{4,0},{8,12},{12,8},{16,20},{20,16},{24,28},{28,24},{1,5},{5... | collective-permute-start | bytes 1572872 | tf_op jit(solution)/shard_map/ppermute | solution.py:14
  95.3 150.4 %all-reduce.7.cloned.1.call-start = ((), (), s32[]{:S(2)}) async-start(), calls=%async_computation.3 | async-start | bytes 1048576 | tf_op jit(solution)/shard_map/psum | solution.py:137
  115.1 4.9 %copy-start.2 = (f32[2,256,512]{2,1,0:T(8,128)S(1)}, f32[2,256,512]{2,1,0:T(8,128)}, u32[]{:S(2)}) copy-start(f32[2,256,512]{2,1,0:T(8,128)} %all-gather.5.cloned.1.call-done) | copy-start | bytes 3145732
  129.5 1.9 slice-start
  197.6 2.6 slice-start.1
  200.1 168.3 %all-reduce.9.cloned.1.call-start = ((), (), s32[]{:S(2)}) async-start(), calls=%async_computation.4 | async-start | bytes 524288 | tf_op jit(solution)/shard_map/psum | solution.py:154
  245.6 8.0 %collective-permute-start.7 = (f32[512,256]{1,0:T(8,128)}, f32[512,256]{1,0:T(8,128)S(1)}, u32[]{:S(2)}, u32[]{:S(2)}) collective-permute-start(f32[512,256]{1,0:T(8,128)} %all-reduce.7.cloned.1.call-done), channel_id=1, source_target_pairs={{0,4},{4,0},{8,12},{12,8},{16,20},{20,16},{24,28},{28,24},{1,5},{5... | collective-permute-start | bytes 1572872 | tf_op jit(solution)/shard_map/ppermute | solution.py:14
  247.4 2.6 copy-start.3
  247.5 6.2 %copy-start.10 = (f32[512,256]{1,0:T(8,128)S(1)}, f32[512,256]{1,0:T(8,128)}, u32[]{:S(2)}) copy-start(f32[512,256]{1,0:T(8,128)} %all-reduce.7.cloned.1.call-done) | copy-start | bytes 1572868
  247.5 8.5 %copy-start.6 = (f32[256,768]{1,0:T(8,128)S(1)}, f32[256,768]{1,0:T(8,128)}, u32[]{:S(2)}) copy-start(f32[256,768]{1,0:T(8,128)} %copy-done.5) | copy-start | bytes 2359300
  250.0 118.4 %collective-permute-start.3 = (f32[4,64,2048]{2,1,0:T(8,128)}, f32[4,64,2048]{2,1,0:T(8,128)}, u32[]{:S(2)}, u32[]{:S(2)}) collective-permute-start(f32[4,64,2048]{2,1,0:T(8,128)} %constant_dynamic-slice_fusion.3), channel_id=1, source_target_pairs={{0,8},{4,12},{8,0},{12,4},{16,24},{20,28},{24,16},{28,20},{1,9},{5... | collective-permute-start | bytes 6291464 | tf_op jit(solution)/shard_map/ppermute | solution.py:14
  253.1 57.0 %collective-permute-start.6 = (f32[8,64,256]{2,1,0:T(8,128)}, f32[8,64,256]{2,1,0:T(8,128)}, u32[]{:S(2)}, u32[]{:S(2)}) collective-permute-start(f32[8,64,256]{2,1,0:T(8,128)} %add_dynamic-update-slice_fusion), channel_id=1, source_target_pairs={{0,8},{4,12},{8,0},{12,4},{16,24},{20,28},{24,16},{28,20},{1,9},{5... | collective-permute-start | bytes 1572872 | tf_op jit(solution)/shard_map/ppermute | solution.py:14
  254.5 66.3 %collective-permute-start.8 = (f32[512,256]{1,0:T(8,128)}, f32[512,256]{1,0:T(8,128)}, u32[]{:S(2)}, u32[]{:S(2)}) collective-permute-start(f32[512,256]{1,0:T(8,128)} %add.281), channel_id=1, source_target_pairs={{0,8},{4,12},{8,0},{12,4},{16,24},{20,28},{24,16},{28,20},{1,9},{5... | collective-permute-start | bytes 1572872 | tf_op jit(solution)/shard_map/ppermute | solution.py:14
  368.4 4.1 %collective-permute-start.9 = (f32[256,256]{1,0:T(8,128)}, f32[256,256]{1,0:T(8,128)}, u32[]{:S(2)}, u32[]{:S(2)}) collective-permute-start(f32[256,256]{1,0:T(8,128)} %all-reduce.9.cloned.1.call-done), channel_id=1, source_target_pairs={{0,4},{4,0},{8,12},{12,8},{16,20},{20,16},{24,28},{28,24},{1,5},{5... | collective-permute-start | bytes 786440 | tf_op jit(solution)/shard_map/ppermute | solution.py:14
  371.9 3.1 collective-permute-start.4
  372.5 4.9 %copy-start.1 = (f32[4,64,1024]{2,1,0:T(8,128)S(1)}, f32[4,64,1024]{2,1,0:T(8,128)}, u32[]{:S(2)}) copy-start(f32[4,64,1024]{2,1,0:T(8,128)} %param.4) | copy-start | bytes 3145732
Sparse Core Ops, SparseCore 0:
  85.6 26.7 all-gather.4
  114.3 35.1 all-gather.6
  151.9 35.1 all-gather.8
  200.2 45.3 all-reduce.6
  325.3 43.0 all-reduce.8
where the time goes:
time: 385 us; the launch traced here: 384 us
  waiting for transfers between devices  234 us (61%)
  local copies, waits for them, and re-layouts  38.4 us (10%)
  matrix products  32.8 us (9%)
  blocking collectives  32.7 us (8%)
  other arithmetic  19.8 us (5%)
  between operations  19.8 us (5%)
  starting transfers between devices  6.62 us (2%)
    ppermute x10, waiting for transfers between devices, swapped(): return lax.ppermute(value, axis, pairs)  82.2 us
    psum x1, waiting for transfers between devices, shards(): partial_one = lax.psum(partial_one, 'sub')  43.1 us
    psum x1, waiting for transfers between devices, shards(): partial_two = lax.psum(partial_two, 'sub')  39.8 us
    all_gather x1, waiting for transfers between devices, shards(): lax.all_gather(second_node[:, :, :4 * W], 'sub', axis=1, tiled=True)  34.4 us
    dot_general x24, matrix products, exact_dot(): jnp.dot(left_matrix, right_matrix, precision=lax.Precision.HIGHEST, prefe...  32.8 us
    all_gather x1, waiting for transfers between devices, shards(): lax.all_gather(first_node[:, :, :4 * W], 'sub', axis=1, tiled=True)  17.2 us
    all_gather x1, waiting for transfers between devices, interface_inverse(): lax.all_gather(block_rows, 'sub', axis=1, tiled=True)  16.9 us
    all_gather x1, blocking collectives, shards(): lax.all_gather(second_piece[:, :3 * W], 'sub', axis=0, tiled=True)  12.5 us
  transfers between devices with their start and end apart: 15, of which 10 were waited for; matrix products, arithmetic and copies ran while one was open for 18% of the time, Pallas kernels for 0%

commit v1 on v0

--- a/solution.py
+++ b/solution.py
@@ -151,7 +151,7 @@
     )
     node_data = jnp.take(candidates, my_positions, axis=0)
     partial_one = exact_dot(right_one, node_data.reshape(3 * width_local, K))
-    partial_one = lax.psum(partial_one, "sub")
+    partial_one = jnp.sum(lax.all_gather(partial_one, "sub"), axis=0)
     partial_one = partial_one + swapped(partial_one, "leaf", 0)
     inner_one = -exact_dot(inverse_one, partial_one)
     inner_slice = lax.dynamic_slice_in_dim(inner_one, member_index * width_local, width_local, 0)

time: 385 us -> 370 us (0.961)
  waiting for transfers between devices: 234 us -> 215 us
  other arithmetic: 19.8 us -> 24 us
    psum x1 -> x0, waiting for transfers between devices: 43.1 us -> none  [shards(): partial_one = lax.psum(partial_one, 'sub')]
    all_gather x0 -> x1, waiting for transfers between devices: none -> 22.4 us  [shards(): partial_one = jnp.sum(lax.all_gather(partial_one, 'sub'), axis=0)]
  transfers between devices with their start and end apart: 15 -> 15, of which waited for: 10 -> 9; matrix products, arithmetic and copies ran while one was open for 18% -> 20% of each run, Pallas kernels for 0% -> 0%
where the time goes in v1:
time: 370 us; the launch traced here: 369 us
  waiting for transfers between devices  215 us (58%)
  local copies, waits for them, and re-layouts  39.9 us (11%)
  blocking collectives  32.7 us (9%)
  matrix products  31.7 us (9%)
  other arithmetic  24 us (6%)
  between operations  19.7 us (5%)
  starting transfers between devices  6.11 us (2%)
    ppermute x10, waiting for transfers between devices, swapped(): return lax.ppermute(value, axis, pairs)  81.9 us
    psum x1, waiting for transfers between devices, shards(): partial_two = lax.psum(partial_two, 'sub')  41.7 us
    all_gather x1, waiting for transfers between devices, shards(): lax.all_gather(second_node[:, :, :4 * W], 'sub', axis=1, tiled=True)  34.4 us
    dot_general x24, matrix products, exact_dot(): jnp.dot(left_matrix, right_matrix, precision=lax.Precision.HIGHEST, prefe...  31.7 us
    all_gather x1, waiting for transfers between devices, shards(): partial_one = jnp.sum(lax.all_gather(partial_one, 'sub'), axis=0)  22.4 us
    all_gather x1, waiting for transfers between devices, shards(): lax.all_gather(first_node[:, :, :4 * W], 'sub', axis=1, tiled=True)  17.2 us
    all_gather x1, waiting for transfers between devices, interface_inverse(): lax.all_gather(block_rows, 'sub', axis=1, tiled=True)  16.9 us
    all_gather x1, blocking collectives, shards(): lax.all_gather(second_piece[:, :3 * W], 'sub', axis=0, tiled=True)  12.5 us
  transfers between devices with their start and end apart: 15, of which 9 were waited for; matrix products, arithmetic and copies ran while one was open for 20% of the time, Pallas kernels for 0%

profile of v1, /device:TPU:0, one launch (start us, length us, event | category | flops | bytes accessed | tf_op | source)
XLA Modules:
  0.0 368.6 jit_solution(12519616926999069865)
XLA Ops:
  13.0 10.0 %all-gather = f32[256,256]{1,0:T(8,128)S(1)} all-gather(f32[64,256]{1,0:T(8,128)S(1)} %slice_add_fusion.1), channel_id=2, replica_groups=mesh['leaf'=8,'sub'=4] {'sub'}, dimensions={0}, use_global_device_ids=true | all-gather | bytes 327680 | tf_op jit(solution)/shard_map/all_gather | solution.py:28
  27.6 12.5 %all_gather.26 = f32[256,768]{1,0:T(8,128)S(1)} all-gather(f32[64,768]{1,0:T(8,128)S(1)} %slice.143), channel_id=1, replica_groups=mesh['leaf'=8,'sub'=4] {'sub'}, dimensions={0}, use_global_device_ids=true | all-gather | bytes 983040 | tf_op jit(solution)/shard_map/all_gather | solution.py:60
  40.0 10.2 %all_gather.25 = f32[256,768]{1,0:T(8,128)S(1)} all-gather(f32[64,768]{1,0:T(8,128)S(1)} %slice.142), channel_id=1, replica_groups=mesh['leaf'=8,'sub'=4] {'sub'}, dimensions={0}, use_global_device_ids=true | all-gather | bytes 983040 | tf_op jit(solution)/shard_map/all_gather | solution.py:59
  50.6 1.2 convolution_subtract_fusion
  51.8 1.5 reshape_reshape.3
  53.3 2.8 copy.20
  56.1 1.9 gather_fusion.3
  59.1 2.3 collective-permute-done.1
  61.4 1.0 fusion.90
  62.4 1.6 collective-permute-start.2
  64.0 18.3 %collective-permute-done.2 = f32[2,64,1536]{2,1,0:T(8,128)} collective-permute-done((f32[2,64,1536]{2,1,0:T(8,128)}, f32[2,64,1536]{2,1,0:T(8,128)}, u32[]{:S(2)}, u32[]{:S(2)}) %collective-permute-start.2) | collective-permute-done | bytes 786464 | tf_op jit(solution)/shard_map/ppermute | solution.py:14
  82.3 1.5 broadcast_select_fusion.3
  85.5 1.9 slice.148
  95.5 16.9 %all-gather.7.cloned.1.call-done = f32[2,256,512]{2,1,0:T(8,128)} async-done(((f32[2,64,512]{2,1,0:T(8,128)}), f32[2,256,512]{2,1,0:T(8,128)}) %all-gather.7.cloned.1.call-update) | async-done | bytes 1048592 | tf_op jit(solution)/shard_map/all_gather | solution.py:28
  112.4 1.4 abs_reduce_fusion
  115.1 3.1 fusion.2
  118.2 1.8 fusion.7
  120.0 1.8 fusion.45
  121.8 1.8 convolution_subtract_fusion.4
  123.7 1.8 fusion.46
  125.5 1.8 convolution_subtract_fusion.3
  127.4 2.1 fusion.47
  129.5 1.9 convolution_subtract_fusion.2
  132.2 17.2 %all-gather.9.cloned.1.call-done = f32[2,256,1024]{2,1,0:T(8,128)} async-done(((f32[2,64,1024]{2,1,0:T(8,128)}), f32[2,256,1024]{2,1,0:T(8,128)}) %all-gather.9.cloned.1.call-update) | async-done | bytes 2097168 | tf_op jit(solution)/shard_map/all_gather | solution.py:103
  149.4 3.3 constant_dynamic-update-slice_fusion.1
  152.7 34.4 %all-gather.11.cloned.1.call-done = f32[2,256,1024]{2,1,0:T(8,128)} async-done(((f32[2,64,1024]{2,1,0:T(8,128)}), f32[2,256,1024]{2,1,0:T(8,128)}) %all-gather.11.cloned.1.call-update) | async-done | bytes 2097168 | tf_op jit(solution)/shard_map/all_gather | solution.py:104
  187.1 3.3 constant_dynamic-update-slice_fusion
  190.4 7.4 %copy.24 = f32[2,256,2048]{1,0,2:T(2,128)} copy(f32[2,256,2048]{2,1,0:T(8,128)} %constant_dynamic-update-slice_fusion) | data formatting | bytes 8388608 | tf_op jit(solution)/shard_map/reshape | solution.py:110
  197.7 4.7 %convolution_subtract_fusion.1 = f32[192,2048]{1,0:T(8,128)S(1)} fusion(f32[192,512]{1,0:T(8,128)S(1)} %fusion.48, f32[512,2048]{1,0:T(8,128)} %bitcast.130, f32[192,1024]{1,0:T(8,128)S(1)} %bitcast.132, pred[]{:T(512)S(6)} %eq.94), kind=kOutput, calls=%fused_computation.8 | convolution fusion | flops 2416705536 | bytes 6946817 | tf_op jit(solution)/shard_map/dot_general | solution.py:18
  204.4 1.4 fusion.49
  205.8 3.7 %multiply_add_fusion = f32[8,64,2048]{2,1,0:T(8,128)} fusion(f32[64,2048]{1,0:T(8,128)S(1)} %get-tuple-element.7, f32[8]{0:T(128)S(1)} %get-tuple-element.27, f32[64,2048]{1,0:T(8,128)} %get-tuple-element.8, f32[8]{0:T(128)S(1)} %get-tuple-element.28, f32[64,2048]{1,0:T(8,128)S(1)} %get-tuple-element.6, f32[8]{0:T(128)S(1)} %and_convert_fusion.2), kind=kLoop, calls=%fused_computation.6 | loop fusion | flops 5242880 | bytes 5767264 | tf_op jit(solution)/shard_map/add | solution.py:126
  209.6 41.7 %all-reduce.6.cloned.1.call-done = f32[512,256]{1,0:T(8,128)} async-done(((f32[512,256]{1,0:T(8,128)}), f32[512,256]{1,0:T(8,128)}) %all-reduce.6.cloned.1.call-update) | async-done | bytes 524304 | tf_op jit(solution)/shard_map/psum | solution.py:137
  251.3 3.3 constant_dynamic-slice_fusion.3
  254.6 1.5 collective-permute-start.3
  256.1 1.6 add_dynamic-update-slice_fusion
  259.2 1.5 collective-permute-start.8
  260.7 1.0 broadcast_select_fusion.1
  261.7 1.4 copy.23
  263.1 51.6 %collective-permute-done.6 = f32[8,64,256]{2,1,0:T(8,128)} collective-permute-done((f32[8,64,256]{2,1,0:T(8,128)}, f32[8,64,256]{2,1,0:T(8,128)}, u32[]{:S(2)}, u32[]{:S(2)}) %collective-permute-start.6) | collective-permute-done | bytes 524320 | tf_op jit(solution)/shard_map/ppermute | solution.py:14
  314.7 1.1 dynamic-slice_add_fusion.2
  315.7 9.7 %collective-permute-done.8 = f32[512,256]{1,0:T(8,128)} collective-permute-done((f32[512,256]{1,0:T(8,128)}, f32[512,256]{1,0:T(8,128)}, u32[]{:S(2)}, u32[]{:S(2)}) %collective-permute-start.8) | collective-permute-done | bytes 524320 | tf_op jit(solution)/shard_map/ppermute | solution.py:14
  325.4 2.2 convolution_negate_fusion
  328.3 1.4 convolution_bitcast_fusion
  329.7 2.5 dynamic-slice_add_fusion
  332.2 1.0 constant_dynamic-slice_fusion.2
  334.0 22.4 %all-gather.13.cloned.1.call-done = f32[1024,256]{1,0:T(8,128)} async-done(((f32[256,256]{1,0:T(8,128)}), f32[1024,256]{1,0:T(8,128)}) %all-gather.13.cloned.1.call-update) | async-done | bytes 1048592 | tf_op jit(solution)/shard_map/all_gather | solution.py:154
  356.4 2.1 reduce_sum.39
  358.5 2.4 dynamic-slice_add_fusion.1
  (122 shorter events, 24.2 us)
Async XLA Ops:
  7.2 1.2 copy-start
  7.2 105.2 %all-gather.7.cloned.1.call-start = ((), (), s32[]{:S(2)}) async-start(), calls=%async_computation | async-start | bytes 1310720 | tf_op jit(solution)/shard_map/all_gather | solution.py:28
  10.3 2.6 collective-permute-start
  26.8 23.8 %copy-start.7 = (f32[3,64,768]{2,1,0:T(8,128)S(1)}, f32[3,64,768]{2,1,0:T(8,128)}, u32[]{:S(2)}) copy-start(f32[3,64,768]{2,1,0:T(8,128)} %slice.137) | copy-start | bytes 1769476
  50.2 1.6 copy-start.4
  58.3 37.2 %copy-start.3 = (f32[3,64,1536]{2,1,0:T(8,128)}, f32[3,64,1536]{2,1,0:T(8,128)S(1)}, u32[]{:S(2)}) copy-start(f32[3,64,1536]{2,1,0:T(8,128)S(1)} %broadcast_select_fusion) | copy-start | bytes 3538948
  59.0 2.4 collective-permute-start.1
  62.4 19.9 %collective-permute-start.2 = (f32[2,64,1536]{2,1,0:T(8,128)}, f32[2,64,1536]{2,1,0:T(8,128)}, u32[]{:S(2)}, u32[]{:S(2)}) collective-permute-start(f32[2,64,1536]{2,1,0:T(8,128)} %fusion.90), channel_id=1, source_target_pairs={{0,8},{4,12},{8,0},{12,4},{16,24},{20,28},{24,16},{28,20},{1,9},{5... | collective-permute-start | bytes 2359304 | tf_op jit(solution)/shard_map/ppermute | solution.py:14
  83.8 0.9 copy-start.6
  83.8 4.5 %copy-start.8 = (f32[2,64,256]{2,1,0:T(8,128)S(1)}, f32[2,64,256]{2,1,0:T(8,128)}, u32[]{:S(2)}) copy-start(f32[2,64,256]{2,1,0:T(8,128)} %param.7) | copy-start | bytes 393220
  85.5 64.0 %all-gather.9.cloned.1.call-start = ((), (), s32[]{:S(2)}) async-start(), calls=%async_computation.1 | async-start | bytes 2621440 | tf_op jit(solution)/shard_map/all_gather | solution.py:103
  87.4 99.7 %all-gather.11.cloned.1.call-start = ((), (), s32[]{:S(2)}) async-start(), calls=%async_computation.2 | async-start | bytes 2621440 | tf_op jit(solution)/shard_map/all_gather | solution.py:104
  89.0 167.1 %collective-permute-start.5 = (f32[8,64,256]{2,1,0:T(8,128)}, f32[8,64,256]{2,1,0:T(8,128)}, u32[]{:S(2)}, u32[]{:S(2)}) collective-permute-start(f32[8,64,256]{2,1,0:T(8,128)} %constant_dynamic-update-slice_fusion.2), channel_id=1, source_target_pairs={{0,4},{4,0},{8,12},{12,8},{16,20},{20,16},{24,28},{28,24},{1,5},{5... | collective-permute-start | bytes 1572872 | tf_op jit(solution)/shard_map/ppermute | solution.py:14
  95.2 156.1 %all-reduce.6.cloned.1.call-start = ((), (), s32[]{:S(2)}) async-start(), calls=%async_computation.3 | async-start | bytes 1048576 | tf_op jit(solution)/shard_map/psum | solution.py:137
  115.1 4.9 %copy-start.2 = (f32[2,256,512]{2,1,0:T(8,128)S(1)}, f32[2,256,512]{2,1,0:T(8,128)}, u32[]{:S(2)}) copy-start(f32[2,256,512]{2,1,0:T(8,128)} %all-gather.7.cloned.1.call-done) | copy-start | bytes 3145732
  129.5 1.9 slice-start
  190.4 7.4 %slice-start.1 = ((f32[3,64,1536]{2,1,0:T(8,128)}), f32[3,64,1024]{2,1,0:T(8,128)S(1)}, s32[]{:S(2)}) async-start(f32[3,64,1536]{2,1,0:T(8,128)} %copy-done.3), calls=%async_computation.6 | async-start | bytes 1572864 | tf_op jit(solution)/shard_map/slice | solution.py:113
  205.8 150.6 %all-gather.13.cloned.1.call-start = ((), (), s32[]{:S(2)}) async-start(), calls=%async_computation.4 | async-start | bytes 1310720 | tf_op jit(solution)/shard_map/all_gather | solution.py:154
  209.6 51.1 %copy-start.5 = (f32[256,768]{1,0:T(8,128)S(1)}, f32[256,768]{1,0:T(8,128)}, u32[]{:S(2)}) copy-start(f32[256,768]{1,0:T(8,128)} %copy-done.4) | copy-start | bytes 2359300
  251.3 6.9 %copy-start.10 = (f32[512,256]{1,0:T(8,128)S(1)}, f32[512,256]{1,0:T(8,128)}, u32[]{:S(2)}) copy-start(f32[512,256]{1,0:T(8,128)} %all-reduce.6.cloned.1.call-done) | copy-start | bytes 1572868
  251.3 6.9 %collective-permute-start.7 = (f32[512,256]{1,0:T(8,128)}, f32[512,256]{1,0:T(8,128)S(1)}, u32[]{:S(2)}, u32[]{:S(2)}) collective-permute-start(f32[512,256]{1,0:T(8,128)} %all-reduce.6.cloned.1.call-done), channel_id=1, source_target_pairs={{0,4},{4,0},{8,12},{12,8},{16,20},{20,16},{24,28},{28,24},{1,5},{5... | collective-permute-start | bytes 1572872 | tf_op jit(solution)/shard_map/ppermute | solution.py:14
  254.6 75.1 %collective-permute-start.3 = (f32[4,64,2048]{2,1,0:T(8,128)}, f32[4,64,2048]{2,1,0:T(8,128)}, u32[]{:S(2)}, u32[]{:S(2)}) collective-permute-start(f32[4,64,2048]{2,1,0:T(8,128)} %constant_dynamic-slice_fusion.3), channel_id=1, source_target_pairs={{0,8},{4,12},{8,0},{12,4},{16,24},{20,28},{24,16},{28,20},{1,9},{5... | collective-permute-start | bytes 6291464 | tf_op jit(solution)/shard_map/ppermute | solution.py:14
  257.7 57.0 %collective-permute-start.6 = (f32[8,64,256]{2,1,0:T(8,128)}, f32[8,64,256]{2,1,0:T(8,128)}, u32[]{:S(2)}, u32[]{:S(2)}) collective-permute-start(f32[8,64,256]{2,1,0:T(8,128)} %add_dynamic-update-slice_fusion), channel_id=1, source_target_pairs={{0,8},{4,12},{8,0},{12,4},{16,24},{20,28},{24,16},{28,20},{1,9},{5... | collective-permute-start | bytes 1572872 | tf_op jit(solution)/shard_map/ppermute | solution.py:14
  259.2 66.2 %collective-permute-start.8 = (f32[512,256]{1,0:T(8,128)}, f32[512,256]{1,0:T(8,128)}, u32[]{:S(2)}, u32[]{:S(2)}) collective-permute-start(f32[512,256]{1,0:T(8,128)} %add.279), channel_id=1, source_target_pairs={{0,8},{4,12},{8,0},{12,4},{16,24},{20,28},{24,16},{28,20},{1,9},{5... | collective-permute-start | bytes 1572872 | tf_op jit(solution)/shard_map/ppermute | solution.py:14
  333.3 25.2 %collective-permute-start.4 = (f32[2,64,2048]{2,1,0:T(8,128)}, f32[2,64,2048]{2,1,0:T(8,128)}, u32[]{:S(2)}, u32[]{:S(2)}) collective-permute-start(f32[2,64,2048]{2,1,0:T(8,128)} %constant_dynamic-slice_fusion.2), channel_id=1, source_target_pairs={{0,4},{4,0},{8,12},{12,8},{16,20},{20,16},{24,28},{28,24},{1,5},{5... | collective-permute-start | bytes 3145736 | tf_op jit(solution)/shard_map/ppermute | solution.py:14
  356.4 5.8 %copy-start.1 = (f32[4,64,1024]{2,1,0:T(8,128)S(1)}, f32[4,64,1024]{2,1,0:T(8,128)}, u32[]{:S(2)}) copy-start(f32[4,64,1024]{2,1,0:T(8,128)} %param.4) | copy-start | bytes 3145732
  358.5 2.4 copy-start.9
  358.5 2.8 copy-start.11
  358.5 2.4 collective-permute-start.9
Sparse Core Ops, SparseCore 0:
  85.6 26.7 all-gather.6
  114.2 35.1 all-gather.8
  151.9 35.1 all-gather.10
  205.9 45.3 all-reduce.5
  329.8 26.4 all-gather.12
